TPU v7x, 256 devices: a whole 4x4x8 slice. The times are simulated.
256 devices in a mesh: row: 8 (over y, core), col: 32 (over x, z).
Axes of the slice: x: 4, y: 4, z: 8, core: 2. Of those that a mesh axis runs over, the one named last changes fastest.
Arguments:
- columns: float32 [2048, 131072], P(None, ('row', 'col')), may hold values from -6000 to 6000
- seating: int32 [32], replicated, may hold values from 0 to 31, each once
Outputs:
- rotated: float32 [2048, 131072], P(None, ('row', 'col'))
All inputs are finite; a program needn't handle non-finite values.
Results may differ from a plain program's by a relative error of at most 0.0001.
Values sent between devices are 32-bit elements; how exact they have to be, the bound alone decides.
No kernel may reach another device: no remote copies, remote signals or barrier semaphores. Data moves between devices by JAX's collectives and lax.ppermute only.
A program may use at most 128 MiB of HBM per device.

v0:
```python
import jax
import jax.numpy as jnp
from jax import lax
from jax.sharding import PartitionSpec as P

BLOCK = 64
NS_STEPS = 5
highest = lax.Precision.HIGHEST


def rotation(pair_gram, total_rows):
    pair_width = pair_gram.shape[-1]
    frobenius = jnp.sqrt(jnp.sum(pair_gram * pair_gram, axis=(-2, -1), keepdims=True))
    current = pair_gram / frobenius
    identity = jnp.eye(pair_width, dtype=jnp.float32)
    inverse_root = jnp.broadcast_to(identity, pair_gram.shape)
    for newton_turn in range(NS_STEPS):
        factor = 1.5 * identity - 0.5 * jnp.matmul(inverse_root, current, precision=highest)
        current = jnp.matmul(current, factor, precision=highest)
        inverse_root = jnp.matmul(factor, inverse_root, precision=highest)
    return inverse_root * jnp.sqrt(total_rows / frobenius)


def pair_up(blocks, stride):
    count = blocks.shape[0]
    shaped = blocks.reshape(count // (2 * stride), 2, stride, blocks.shape[1], blocks.shape[2])
    return jnp.concatenate([shaped[:, 0], shaped[:, 1]], axis=2)


def split_pairs(rotated_pairs, stride):
    groups = rotated_pairs.shape[0]
    half_width = rotated_pairs.shape[2] // 2
    shaped = rotated_pairs.reshape(groups, stride, 2, half_width, rotated_pairs.shape[3])
    return jnp.transpose(shaped, (0, 2, 1, 3, 4)).reshape(
        groups * 2 * stride, half_width, rotated_pairs.shape[3]
    )


def body(columns, seating):
    block_count = seating.shape[0]
    rows_here = columns.shape[1]
    col_count = lax.axis_size("col")
    total_rows = float(rows_here * lax.axis_size("row") * col_count)
    seat_count = block_count // col_count
    seated = columns.reshape(block_count, BLOCK, rows_here)[seating].reshape(
        block_count * BLOCK, rows_here
    )
    current = seated.reshape(block_count, BLOCK, rows_here)
    for stride in (seat_count, block_count // 2):
        paired = pair_up(current, stride)
        partial_gram = jnp.einsum("gsam,gsbm->gsab", paired, paired, precision=highest)
        pair_gram = lax.psum(partial_gram, ("row", "col"))
        rotate = rotation(pair_gram, total_rows)
        moved = jnp.einsum("gsab,gsam->gsbm", rotate, paired, precision=highest)
        current = split_pairs(moved, stride)
    seated = current.reshape(block_count * BLOCK, rows_here)
    ordered = seated.reshape(block_count, BLOCK, rows_here)
    restored = jnp.zeros_like(ordered).at[seating].set(ordered)
    return restored.reshape(block_count * BLOCK, rows_here)


def solution(mesh):
    in_specs = (P(None, ("row", "col")), P())
    out_specs = P(None, ("row", "col"))
    return jax.shard_map(body, mesh=mesh, in_specs=in_specs, out_specs=out_specs, check_vma=False)
```

profile of v0, /device:TPU:2, one launch (start us, length us, event | category | flops | bytes accessed | tf_op | source)
XLA Modules:
  0.0 617.4 jit_solution(11122427788383581620)
XLA Ops:
  7.2 5.0 gather_fusion
  12.2 2.7 slice_bitcast_fusion.3
  15.0 1.3 copy-done
  16.3 5.0 fusion.4
  21.6 261.7 %all-reduce.3.cloned.1.call-done = f32[16,1,128,128]{3,2,0,1:T(8,128)} async-done(((f32[16,1,128,128]{3,2,0,1:T(8,128)}), f32[16,1,128,128]{3,2,0,1:T(8,128)}) %all-reduce.3.cloned.1.call-update) | async-done | bytes 1048592 | tf_op jit(solution)/shard_map/psum | solution.py:52
  283.3 1.5 multiply_reduce_fusion.1
  284.9 2.3 fusion.15
  288.2 1.3 fusion.19
  289.5 1.2 fusion.14
  290.7 1.2 fusion.35
  293.1 1.2 fusion.13
  295.5 1.2 fusion.36
  296.7 1.4 fusion.12
  300.6 1.2 fusion.11
  301.8 1.9 convolution_multiply_fusion.6
  303.7 3.8 fusion.2
  308.0 1.3 copy-done.2
  309.3 5.5 fusion.5
  314.8 257.9 %all-reduce.5.cloned.1.call-done = f32[1,16,128,128]{3,2,1,0:T(8,128)} async-done(((f32[1,16,128,128]{3,2,1,0:T(8,128)}), f32[1,16,128,128]{3,2,1,0:T(8,128)}) %all-reduce.5.cloned.1.call-update) | async-done | bytes 1048592 | tf_op jit(solution)/shard_map/psum | solution.py:52
  572.8 1.5 multiply_reduce_fusion
  574.3 2.3 fusion.10
  577.7 1.3 fusion.16
  579.0 1.2 fusion.9
  582.6 1.2 fusion.8
  585.0 1.4 fusion.42
  586.3 1.2 fusion.7
  590.0 1.2 fusion.6
  591.2 1.9 convolution_multiply_fusion
  593.1 3.8 fusion
  596.9 2.6 copy.5
  599.5 2.5 broadcast_in_dim.4
  602.1 8.3 %scatter_fusion = f32[32,64,512]{2,1,0:T(8,128)} fusion(f32[32,64,512]{2,1,0:T(8,128)} %broadcast_in_dim.4, s32[32]{0:T(128)S(1)} %compare_select_fusion, f32[32,64,512]{2,1,0:T(8,128)} %bitcast.98), kind=kCustom, calls=%fused_computation.1 | custom fusion | bytes 12583040 | tf_op jit(solution)/shard_map/scatter | solution.py:58
  (32 shorter events, 14.2 us)
Async XLA Ops:
  6.5 276.8 %all-reduce.3.cloned.1.call-start = ((), (), s32[]{:S(2)}) async-start(), calls=%async_computation | async-start | bytes 2097152 | tf_op jit(solution)/shard_map/psum | solution.py:52
  15.0 1.3 copy-start
  21.3 551.4 %all-reduce.5.cloned.1.call-start = ((), (), s32[]{:S(2)}) async-start(), calls=%async_computation.1 | async-start | bytes 2097152 | tf_op jit(solution)/shard_map/psum | solution.py:52
  283.3 4.9 copy-start.4
  299.4 4.3 copy-start.1
  308.0 1.3 copy-start.2
  572.8 4.9 copy-start.5
  588.8 4.3 copy-start.3
Sparse Core Ops, SparseCore 0:
  21.4 261.8 all-reduce.2
  315.0 257.7 all-reduce.4
where the time goes:
time: 622 us; the launch traced here: 617 us
  waiting for transfers between devices  520 us (84%)
  matrix products  55.4 us (9%)
  local copies, waits for them, and re-layouts  24.4 us (4%)
  between operations  13.9 us (2%)
    psum x2, waiting for transfers between devices, body(): pair_gram = lax.psum(partial_gram, ('row', 'col'))  520 us
    dot_general x10, matrix products, rotation(): jnp.matmul(inverse_root, current, precision=highest)  14.6 us
    dot_general x10, matrix products, rotation(): inverse_root = jnp.matmul(factor, inverse_root, precision=highest)  13.1 us
  transfers between devices with their start and end apart: 2, of which 2 were waited for; matrix products, arithmetic and copies ran while one was open for 0% of the time, Pallas kernels for 0%

commit v1 on v0

--- a/solution.py
+++ b/solution.py
@@ -49,7 +49,7 @@
     for stride in (seat_count, block_count // 2):
         paired = pair_up(current, stride)
         partial_gram = jnp.einsum("gsam,gsbm->gsab", paired, paired, precision=highest)
-        pair_gram = lax.psum(partial_gram, ("row", "col"))
+        pair_gram = lax.psum(lax.psum(partial_gram, axis_name="row"), "col")
         rotate = rotation(pair_gram, total_rows)
         moved = jnp.einsum("gsab,gsam->gsbm", rotate, paired, precision=highest)
         current = split_pairs(moved, stride)

time: 622 us -> 544 us (0.87)
  waiting for transfers between devices: 520 us -> 441 us
    psum x2 -> x4, waiting for transfers between devices: 520 us -> 441 us  [body(): pair_gram = lax.psum(lax.psum(partial_gram, axis_name='row'), 'col')]
  transfers between devices with their start and end apart: 2 -> 4, of which waited for: 2 -> 4; matrix products, arithmetic and copies ran while one was open for 0% -> 0% of each run, Pallas kernels for 0% -> 0%
where the time goes in v1:
time: 544 us; the launch traced here: 538 us
  waiting for transfers between devices  441 us (81%)
  matrix products  55.3 us (10%)
  local copies, waits for them, and re-layouts  24.4 us (4%)
  between operations  13.7 us (3%)
    psum x4, waiting for transfers between devices, body(): pair_gram = lax.psum(lax.psum(partial_gram, axis_name='row'), 'col')  441 us
    dot_general x10, matrix products, rotation(): jnp.matmul(inverse_root, current, precision=highest)  15 us
    dot_general x10, matrix products, rotation(): inverse_root = jnp.matmul(factor, inverse_root, precision=highest)  13 us
  transfers between devices with their start and end apart: 4, of which 4 were waited for; matrix products, arithmetic and copies ran while one was open for 0% of the time, Pallas kernels for 0%

profile of v1, /device:TPU:2, one launch (start us, length us, event | category | flops | bytes accessed | tf_op | source)
XLA Modules:
  0.0 538.1 jit_solution(4107555459800619245)
XLA Ops:
  7.2 5.0 gather_fusion
  12.2 2.7 slice_bitcast_fusion.3
  15.0 1.3 copy-done
  16.3 5.0 fusion.4
  21.4 70.9 %all-reduce.5.cloned.1.call-done = f32[16,1,128,128]{3,2,0,1:T(8,128)} async-done(((f32[16,1,128,128]{3,2,0,1:T(8,128)}), f32[16,1,128,128]{3,2,0,1:T(8,128)}) %all-reduce.5.cloned.1.call-update) | async-done | bytes 1048592 | tf_op jit(solution)/shard_map/psum | solution.py:52
  92.5 151.5 %all-reduce.7.cloned.1.call-done = f32[16,1,128,128]{3,2,0,1:T(8,128)} async-done(((f32[16,1,128,128]{3,2,0,1:T(8,128)}), f32[16,1,128,128]{3,2,0,1:T(8,128)}) %all-reduce.7.cloned.1.call-update) | async-done | bytes 1048592 | tf_op jit(solution)/shard_map/psum | solution.py:52
  244.0 1.5 multiply_reduce_fusion.1
  245.6 2.3 fusion.15
  249.0 1.3 fusion.19
  250.2 1.2 fusion.14
  253.8 1.2 fusion.13
  255.1 1.2 fusion.37
  257.5 1.6 fusion.12
  261.5 1.2 fusion.11
  262.7 1.9 convolution_multiply_fusion.6
  264.6 3.8 fusion.2
  268.9 1.3 copy-done.2
  270.2 5.2 fusion.5
  275.5 66.6 %all-reduce.9.cloned.1.call-done = f32[1,16,128,128]{3,2,1,0:T(8,128)} async-done(((f32[1,16,128,128]{3,2,1,0:T(8,128)}), f32[1,16,128,128]{3,2,1,0:T(8,128)}) %all-reduce.9.cloned.1.call-update) | async-done | bytes 1048592 | tf_op jit(solution)/shard_map/psum | solution.py:52
  342.1 151.6 %all-reduce.11.cloned.1.call-done = f32[1,16,128,128]{3,2,1,0:T(8,128)} async-done(((f32[1,16,128,128]{3,2,1,0:T(8,128)}), f32[1,16,128,128]{3,2,1,0:T(8,128)}) %all-reduce.11.cloned.1.call-update) | async-done | bytes 1048592 | tf_op jit(solution)/shard_map/psum | solution.py:52
  493.7 1.5 multiply_reduce_fusion
  495.3 2.3 fusion.10
  498.7 1.3 fusion.16
  499.9 1.2 fusion.9
  503.6 1.2 fusion.8
  507.2 1.4 fusion.7
  511.0 1.2 fusion.6
  512.2 1.9 convolution_multiply_fusion
  514.1 3.8 fusion
  517.9 2.6 copy.5
  520.5 2.5 broadcast_in_dim.4
  523.1 8.3 %scatter_fusion = f32[32,64,512]{2,1,0:T(8,128)} fusion(f32[32,64,512]{2,1,0:T(8,128)} %broadcast_in_dim.4, s32[32]{0:T(128)S(1)} %compare_select_fusion, f32[32,64,512]{2,1,0:T(8,128)} %bitcast.98), kind=kCustom, calls=%fused_computation.1 | custom fusion | bytes 12583040 | tf_op jit(solution)/shard_map/scatter | solution.py:58
  (38 shorter events, 16.7 us)
Async XLA Ops:
  6.5 85.7 %all-reduce.5.cloned.1.call-start = ((), (), s32[]{:S(2)}) async-start(), calls=%async_computation | async-start | bytes 2097152 | tf_op jit(solution)/shard_map/psum | solution.py:52
  15.0 1.3 copy-start
  21.3 222.7 %all-reduce.7.cloned.1.call-start = ((), (), s32[]{:S(2)}) async-start(), calls=%async_computation.1 | async-start | bytes 2097152 | tf_op jit(solution)/shard_map/psum | solution.py:52
  92.2 249.8 %all-reduce.9.cloned.1.call-start = ((), (), s32[]{:S(2)}) async-start(), calls=%async_computation.2 | async-start | bytes 2097152 | tf_op jit(solution)/shard_map/psum | solution.py:52
  244.0 4.9 copy-start.4
  260.3 4.3 copy-start.1
  268.9 1.3 copy-start.2
  275.5 218.3 %all-reduce.11.cloned.1.call-start = ((), (), s32[]{:S(2)}) async-start(), calls=%async_computation.3 | async-start | bytes 2097152 | tf_op jit(solution)/shard_map/psum | solution.py:52
  493.7 4.9 copy-start.5
  509.8 4.3 copy-start.3
Sparse Core Ops, SparseCore 0:
  21.4 70.7 all-reduce.4
  95.7 148.3 all-reduce.6
  275.6 66.4 all-reduce.8
  345.4 148.3 all-reduce.10
